TPU v7x, 128 devices: a whole 4x4x4 slice. The times are simulated.
128 devices in a mesh: view: 4 (over x), xy: 16 (over z, y), gz: 2 (over core).
Axes of the slice: x: 4, y: 4, z: 4, core: 2. Of those that a mesh axis runs over, the one named last changes fastest.
Arguments:
- estimate: float32 [64, 1024, 128], P('gz', 'xy'), may hold values from 0.5 to 2
- views: bfloat16 [4, 64, 1024, 128], P('view', 'gz', 'xy'), may hold values from 0.19921875 to 3
- shifts: int32 [4, 3], P('view'), may hold values from -32 to 32, as said below
- kernels: float32 [4, 3, 63], P('view'), may hold values from 0.02 to 1
- coverage: int32 [4, 8, 1], replicated, may hold values from 0 to 1, as said below
Outputs:
- refined: float32 [64, 1024, 128], P('gz', 'xy')
Inputs may be any that keep to these rules, and one draw needn't show every extreme that they name: `shifts`: both ends -32 and 32 occur in every draw. `coverage`: every block is covered by at least one view.
All inputs are finite; a program needn't handle non-finite values.
Results may differ from a plain program's by a relative error of at most 0.0003.
Values may be sent and summed in bfloat16 or wider, within the bound.
No kernel may reach another device: no remote copies, remote signals or barrier semaphores. Data moves between devices by JAX's collectives and lax.ppermute only.
A program may use at most 64 MiB of HBM per device.

v0:
```python
import jax
import jax.numpy as jnp
from jax import lax
from jax.sharding import PartitionSpec as P

SHIFT = 32
BLOCK = 128
ITERS = 2


def shortened(shard):

    def short(part):
        return part.astype(jnp.bfloat16) if part.dtype == jnp.float32 else part

    return jax.tree.map(short, shard)


def extended(cells, sides, width):
    for axis, dim in sides:
        count = lax.axis_size(axis)
        ends = count - 1
        head = lax.slice_in_dim(cells, 0, width, axis=dim)
        tail = lax.slice_in_dim(cells, cells.shape[dim] - width, cells.shape[dim], axis=dim)
        cells = jnp.concatenate(
            [
                lax.ppermute(tail, axis, [(i, (i + 1) % count) for i in range(ends)]),
                cells,
                lax.ppermute(head, axis, [((i + 1) % count, i) for i in range(ends)]),
            ],
            axis=dim,
        )
    return cells


def band(kern, rows, cols, offset):
    row_ids = lax.broadcasted_iota(jnp.int32, (rows, cols), 0)
    col_ids = lax.broadcasted_iota(jnp.int32, (rows, cols), 1)
    offsets = row_ids - col_ids + offset

    def add_tap(tap_index, summed):
        return summed + jnp.where(offsets == tap_index, kern[tap_index], 0.0)

    return lax.fori_loop(0, kern.shape[0], add_tap, jnp.zeros((rows, cols), jnp.float32))


def along_x(vol, matrix):
    return jnp.einsum("zyx,xk->zyk", vol, matrix, precision=lax.Precision.HIGHEST)


def banded_rows(piece, matrix, half):
    rows_all = piece.shape[1]
    tile = matrix.shape[1]
    padded = jnp.pad(piece, ((0, 0), (half, half), (0, 0)))
    blocks = rows_all // tile
    windows = jnp.stack(
        [
            lax.slice_in_dim(padded, b * tile, b * tile + tile + 2 * half, axis=1)
            for b in range(blocks)
        ],
        axis=1,
    )
    out = jnp.einsum("zbwx,wk->zbkx", windows, matrix, precision=lax.Precision.HIGHEST)
    return out.reshape(piece.shape[0], rows_all, piece.shape[2])


def along_rows(vol, pencil_mat, half):
    out = banded_rows(
        lax.all_to_all(shortened(vol), "xy", split_axis=0, concat_axis=1, tiled=True).astype(
            vol.dtype
        ),
        pencil_mat,
        half,
    )
    return lax.all_to_all(out, "xy", split_axis=1, concat_axis=0, tiled=True)


def along_planes(vol, matrix, half):
    padded = extended(vol, (("gz", 0),), half)
    return jnp.einsum("zyx,zk->kyx", padded, matrix, precision=lax.Precision.HIGHEST)


def on_device(estimate, views, shifts, kernels, coverage):
    slab, strip, width = estimate.shape
    taps = kernels.shape[2]
    half = (taps - 1) // 2
    tile = 128
    psf = kernels[0] / jnp.sum(kernels[0], axis=1, keepdims=True)
    raw = views[0]
    margin = SHIFT
    padded = extended(raw, (("gz", 0), ("xy", 1)), margin)
    padded = jnp.pad(padded, ((0, 0), (0, 0), (margin, margin)))
    start = margin + shifts[0]
    data = lax.dynamic_slice(padded, (start[0], start[1], start[2]), (slab, strip, width)).astype(
        jnp.float32
    )
    field = estimate
    row_first = lax.axis_index("xy") * strip
    planes = field.shape[0]
    mats = []
    for reverse in (False, True):
        rows_psf = psf[:, ::-1] if reverse else psf
        x_mat = band(rows_psf[2], width, width, half)
        z_mat = band(rows_psf[0], planes + 2 * half, planes, 0)
        y_mat = band(rows_psf[1], tile + 2 * half, tile, 0)
        mats.append((x_mat, y_mat, None, z_mat))
    row_global = row_first + lax.broadcasted_iota(jnp.int32, (strip,), 0)
    row_onehot = (row_global[:, None] // BLOCK == jnp.arange(coverage.shape[1])[None]).astype(
        jnp.float32
    )
    col_onehot = (
        jnp.arange(width)[:, None] // BLOCK == jnp.arange(coverage.shape[2])[None]
    ).astype(jnp.float32)
    grid = jnp.einsum("vbc,yb,xc->vyx", coverage.astype(jnp.float32), row_onehot, col_onehot)
    mine = lax.dynamic_index_in_dim(grid, lax.axis_index("view"), 0, keepdims=False)
    count = jnp.sum(grid, axis=0)
    for step in range(ITERS):
        predicted = along_x(field, mats[0][0])
        predicted = along_rows(predicted, mats[0][1], half)
        predicted = along_planes(predicted, mats[0][3], half)
        ratio = data / (predicted + 0.05)
        back = along_x(ratio, mats[1][0])
        back = along_rows(back, mats[1][1], half)
        back = along_planes(back, mats[1][3], half)
        term = mine[None] * back
        total = lax.psum(term, "view")
        field = field * total / count[None]
    return field


def solution(mesh):
    placed = (
        P("gz", "xy", None),
        P("view", "gz", "xy", None),
        P("view", None),
        P("view", None, None),
        P(),
    )
    return jax.shard_map(
        on_device, mesh=mesh, in_specs=placed, out_specs=P("gz", "xy", None), check_vma=False
    )
```

profile of v0, /device:TPU:0, one launch (start us, length us, event | category | flops | bytes accessed | tf_op | source)
XLA Modules:
  0.0 838.2 jit_solution(7142134574936693897)
XLA Ops:
  9.3 3.9 collective-permute-start
  14.7 86.1 %while.88 = (s32[]{:T(128)}, f32[128,128]{1,0:T(8,128)S(1)}, f32[63]{0:T(128)S(1)}, s32[]{:T(128)}, s32[]{:T(128)}) while((s32[]{:T(128)}, f32[128,128]{1,0:T(8,128)S(1)}, f32[63]{0:T(128)S(1)}, s32[]{:T(128)}, s32[]{:T(128)}) %tuple.181), condition=%wide.region_10.11_spmd.clone, body=%wide.region_9.10_spmd.clone.sunk | while | flops 98307 | bytes 131171 | solution.py:44
  102.6 8.2 all-to-all-start
  110.8 87.1 %while.87 = (s32[]{:T(128)}, f32[190,128]{1,0:T(8,128)S(1)}, f32[63]{0:T(128)S(1)}, s32[]{:T(128)}, s32[]{:T(128)}) while((s32[]{:T(128)}, f32[190,128]{1,0:T(8,128)S(1)}, f32[63]{0:T(128)S(1)}, s32[]{:T(128)}, s32[]{:T(128)}) %tuple.184), condition=%wide.region_8.9_spmd.clone, body=%wide.region_7.8_spmd.clone.sunk | while | flops 121603 | bytes 194659 | solution.py:44
  198.1 86.6 %while.89 = (s32[]{:T(128)}, f32[128,128]{1,0:T(8,128)S(1)}, f32[63]{0:T(128)S(1)}, s32[]{:T(128)}, s32[]{:T(128)}) while((s32[]{:T(128)}, f32[128,128]{1,0:T(8,128)S(1)}, f32[63]{0:T(128)S(1)}, s32[]{:T(128)}, s32[]{:T(128)}) %tuple.205), condition=%wide.region_12.13_spmd.clone, body=%wide.region_11.12_spmd.clone.sunk | while | flops 98307 | bytes 131171 | solution.py:44
  288.0 7.3 all-to-all-start.1
  295.3 85.6 %while.86 = (s32[]{:T(128)}, f32[94,32]{1,0:T(8,128)S(1)}, f32[63]{0:T(128)S(1)}, s32[]{:T(128)}, s32[]{:T(128)}) while((s32[]{:T(128)}, f32[94,32]{1,0:T(8,128)S(1)}, f32[63]{0:T(128)S(1)}, s32[]{:T(128)}, s32[]{:T(128)}) %tuple.187), condition=%wide.region_6.7_spmd.clone, body=%wide.region_5.6_spmd.clone.sunk | while | flops 15043 | bytes 24163 | solution.py:44
  391.2 5.4 collective-permute-start.2
  398.4 3.7 collective-permute-start.4
  403.7 5.6 collective-permute-done.3
  410.5 5.6 fusion.68
  422.4 9.9 %all-to-all-start.2 = ((bf16[32,64,128]{2,1,0:T(8,128)(2,1)}), bf16[32,64,128]{2,1,0:T(8,128)(2,1)S(1)}, u32[]{:S(2)}, u32[]{:S(2)}) async-start(bf16[32,64,128]{2,1,0:T(8,128)(2,1)} %convolution_convert_fusion.2), calls=%async_computation.2 | async-start | bytes 1048576 | tf_op jit(solution)/shard_map/all_to_all | solution.py:69
  432.3 80.0 %while.85 = (s32[]{:T(128)}, f32[190,128]{1,0:T(8,128)S(1)}, f32[63]{0:T(128)S(1)}, s32[]{:T(128)}, s32[]{:T(128)}) while((s32[]{:T(128)}, f32[190,128]{1,0:T(8,128)S(1)}, f32[63]{0:T(128)S(1)}, s32[]{:T(128)}, s32[]{:T(128)}) %tuple.203), condition=%wide.region_4.5_spmd.clone, body=%wide.region_3.4_spmd.clone.sunk | while | flops 121603 | bytes 194659 | solution.py:44
  515.6 7.3 all-to-all-start.3
  523.1 13.8 %all-to-all-done.3 = f32[2,1024,128]{2,0,1:T(2,128)S(1)} async-done(((f32[2,1024,128]{2,0,1:T(2,128)}), f32[2,1024,128]{2,0,1:T(2,128)S(1)}, u32[]{:S(2)}, u32[]{:S(2)}) %all-to-all-start.3) | async-done | bytes 1048608 | tf_op jit(solution)/shard_map/all_to_all | solution.py:75
  541.2 5.0 collective-permute-start.6
  546.1 87.8 %while.84 = (s32[]{:T(128)}, f32[94,32]{1,0:T(8,128)S(1)}, f32[63]{0:T(128)S(1)}, s32[]{:T(128)}, s32[]{:T(128)}) while((s32[]{:T(128)}, f32[94,32]{1,0:T(8,128)S(1)}, f32[63]{0:T(128)S(1)}, s32[]{:T(128)}, s32[]{:T(128)}) %tuple.204), condition=%wide.region_2.3_spmd.clone, body=%wide.region_1.2_spmd.clone.sunk | while | flops 15043 | bytes 24163 | solution.py:44
  641.0 43.3 %all-reduce.8.cloned.1.call-done = f32[32,64,128]{2,0,1:T(8,128)} async-done(((f32[32,64,128]{2,0,1:T(8,128)}), f32[32,64,128]{2,0,1:T(8,128)}) %all-reduce.8.cloned.1.call-update) | async-done | bytes 1048592 | tf_op jit(solution)/shard_map/psum | solution.py:126
  687.9 17.1 %all_to_all.108 = bf16[32,64,128]{2,1,0:T(8,128)(2,1)S(1)} all-to-all(bf16[32,64,128]{2,1,0:T(8,128)(2,1)S(1)} %convolution_convert_fusion.1), channel_id=1, replica_groups=mesh['view'=4,'xy'=16,'gz'=2] {'xy'}, dimensions={0} | all-to-all | bytes 1048576 | tf_op jit(solution)/shard_map/all_to_all | solution.py:69
  707.3 17.0 %all_to_all.109 = f32[2,1024,128]{2,0,1:T(2,128)S(1)} all-to-all(f32[2,1024,128]{2,0,1:T(2,128)S(1)} %copy.178), channel_id=1, replica_groups=mesh['view'=4,'xy'=16,'gz'=2] {'xy'}, dimensions={1} | all-to-all | bytes 2097152 | tf_op jit(solution)/shard_map/all_to_all | solution.py:75
  726.0 3.2 collective-permute-start.8
  735.6 15.0 %all_to_all.110 = bf16[32,64,128]{2,1,0:T(8,128)(2,1)S(1)} all-to-all(bf16[32,64,128]{2,1,0:T(8,128)(2,1)S(1)} %convolution_convert_fusion), channel_id=1, replica_groups=mesh['view'=4,'xy'=16,'gz'=2] {'xy'}, dimensions={0} | all-to-all | bytes 1048576 | tf_op jit(solution)/shard_map/all_to_all | solution.py:69
  752.9 19.9 %all_to_all.111 = f32[2,1024,128]{2,0,1:T(2,128)S(1)} all-to-all(f32[2,1024,128]{2,0,1:T(2,128)S(1)} %copy.194), channel_id=1, replica_groups=mesh['view'=4,'xy'=16,'gz'=2] {'xy'}, dimensions={1} | all-to-all | bytes 2097152 | tf_op jit(solution)/shard_map/all_to_all | solution.py:75
  784.9 43.2 %all-reduce.10.cloned.1.call-done = f32[32,64,128]{2,0,1:T(8,128)} async-done(((f32[32,64,128]{2,0,1:T(8,128)}), f32[32,64,128]{2,0,1:T(8,128)}) %all-reduce.10.cloned.1.call-update) | async-done | bytes 1048592 | tf_op jit(solution)/shard_map/psum | solution.py:126
  (902 shorter events, 575.1 us)
Async XLA Ops:
  6.5 94.3 %copy-start = (f32[32,64,128]{2,1,0:T(8,128)S(1)}, f32[32,64,128]{2,1,0:T(8,128)}, u32[]{:S(2)}) copy-start(f32[32,64,128]{2,1,0:T(8,128)} %param.17) | copy-start | bytes 3145732
  8.0 379.5 %collective-permute-start.1 = (bf16[32,64,128]{2,0,1:T(8,128)(2,1)S(1)}, bf16[32,64,128]{2,0,1:T(8,128)(2,1)S(1)}, u32[]{:S(2)}, u32[]{:S(2)}) collective-permute-start(bf16[32,64,128]{2,0,1:T(8,128)(2,1)S(1)} %bitcast.354), channel_id=1, source_target_pairs={{1,0},{3,2},{5,4},{7,6},{9,8},{11,10},{13,12},{15,14},{17,16},{19,... | collective-permute-start | bytes 1572872 | tf_op jit(solution)/shard_map/ppermute | solution.py:29
  9.3 378.2 %collective-permute-start = (bf16[32,64,128]{2,0,1:T(8,128)(2,1)S(1)}, bf16[32,64,128]{2,0,1:T(8,128)(2,1)}, u32[]{:S(2)}, u32[]{:S(2)}) collective-permute-start(bf16[32,64,128]{2,0,1:T(8,128)(2,1)S(1)} %bitcast.355), channel_id=1, source_target_pairs={{0,1},{2,3},{4,5},{6,7},{8,9},{10,11},{12,13},{14,15},{16,17},{18,... | collective-permute-start | bytes 1572872 | tf_op jit(solution)/shard_map/ppermute | solution.py:27
  102.6 182.0 %all-to-all-start = ((bf16[32,64,128]{2,1,0:T(8,128)(2,1)}), bf16[32,64,128]{2,1,0:T(8,128)(2,1)S(1)}, u32[]{:S(2)}, u32[]{:S(2)}) async-start(bf16[32,64,128]{2,1,0:T(8,128)(2,1)} %fusion.48), calls=%async_computation | async-start | bytes 1048576 | tf_op jit(solution)/shard_map/all_to_all | solution.py:69
  288.0 93.0 %copy-start.6 = (s32[1,3]{1,0:T(1,128)S(1)}, s32[1,3]{1,0:T(1,128)}, u32[]{:S(2)}) copy-start(s32[1,3]{1,0:T(1,128)} %param.19) | copy-start | bytes 40
  288.0 108.7 %all-to-all-start.1 = ((f32[2,1024,128]{2,0,1:T(2,128)}), f32[2,1024,128]{2,0,1:T(2,128)S(1)}, u32[]{:S(2)}, u32[]{:S(2)}) async-start(f32[2,1024,128]{2,0,1:T(2,128)} %copy.145), calls=%async_computation.1 | async-start | bytes 2097152 | tf_op jit(solution)/shard_map/all_to_all | solution.py:75
  380.9 37.0 %copy-start.1 = (f32[94,32]{1,0:T(8,128)}, f32[94,32]{1,0:T(8,128)S(1)}, u32[]{:S(2)}) copy-start(f32[94,32]{1,0:T(8,128)S(1)} %get-tuple-element.481) | copy-start | bytes 36100
  389.9 19.4 %collective-permute-start.3 = (bf16[96,32,128]{2,0,1:T(8,128)(2,1)}, bf16[96,32,128]{2,0,1:T(8,128)(2,1)}, u32[]{:S(2)}, u32[]{:S(2)}) collective-permute-start(bf16[96,32,128]{2,0,1:T(8,128)(2,1)} %get-tuple-element.606), channel_id=1, source_target_pairs={{2,0},{4,2},{6,4},{8,6},{10,8},{12,10},{14,12},{16,14},{18,16},{20... | collective-permute-start | bytes 2359304 | tf_op jit(solution)/shard_map/ppermute | solution.py:29
  391.2 19.3 %collective-permute-start.2 = (bf16[96,32,128]{2,0,1:T(8,128)(2,1)}, bf16[96,32,128]{2,0,1:T(8,128)(2,1)}, u32[]{:S(2)}, u32[]{:S(2)}) collective-permute-start(bf16[96,32,128]{2,0,1:T(8,128)(2,1)} %get-tuple-element.605), channel_id=1, source_target_pairs={{0,2},{2,4},{4,6},{6,8},{8,10},{10,12},{12,14},{14,16},{16,18},{18... | collective-permute-start | bytes 2359304 | tf_op jit(solution)/shard_map/ppermute | solution.py:27
  397.1 19.7 %collective-permute-start.5 = (f32[31,64,128]{2,1,0:T(8,128)S(1)}, f32[31,64,128]{2,1,0:T(8,128)S(1)}, u32[]{:S(2)}, u32[]{:S(2)}) collective-permute-start(f32[31,64,128]{2,1,0:T(8,128)S(1)} %get-tuple-element.614), channel_id=1, source_target_pairs={{1,0},{3,2},{5,4},{7,6},{9,8},{11,10},{13,12},{15,14},{17,16},{19,... | collective-permute-start | bytes 3047432 | tf_op jit(solution)/shard_map/ppermute | solution.py:29
  398.4 19.0 %collective-permute-start.4 = (f32[31,64,128]{2,1,0:T(8,128)S(1)}, f32[31,64,128]{2,1,0:T(8,128)S(1)}, u32[]{:S(2)}, u32[]{:S(2)}) collective-permute-start(f32[31,64,128]{2,1,0:T(8,128)S(1)} %get-tuple-element.613), channel_id=1, source_target_pairs={{0,1},{2,3},{4,5},{6,7},{8,9},{10,11},{12,13},{14,15},{16,17},{18,... | collective-permute-start | bytes 3047432 | tf_op jit(solution)/shard_map/ppermute | solution.py:27
  422.4 89.9 %all-to-all-start.2 = ((bf16[32,64,128]{2,1,0:T(8,128)(2,1)}), bf16[32,64,128]{2,1,0:T(8,128)(2,1)S(1)}, u32[]{:S(2)}, u32[]{:S(2)}) async-start(bf16[32,64,128]{2,1,0:T(8,128)(2,1)} %convolution_convert_fusion.2), calls=%async_computation.2 | async-start | bytes 1048576 | tf_op jit(solution)/shard_map/all_to_all | solution.py:69
  515.6 21.3 %all-to-all-start.3 = ((f32[2,1024,128]{2,0,1:T(2,128)}), f32[2,1024,128]{2,0,1:T(2,128)S(1)}, u32[]{:S(2)}, u32[]{:S(2)}) async-start(f32[2,1024,128]{2,0,1:T(2,128)} %copy.161), calls=%async_computation.3 | async-start | bytes 2097152 | tf_op jit(solution)/shard_map/all_to_all | solution.py:75
  522.9 161.4 %all-reduce.8.cloned.1.call-start = ((), (), s32[]{:S(2)}) async-start(), calls=%async_computation.8 | async-start | bytes 2097152 | tf_op jit(solution)/shard_map/psum | solution.py:126
  538.3 95.7 %copy-start.5 = (s32[4,8,1]{1,2,0:T(1,128)S(1)}, s32[4,8,1]{1,2,0:T(1,128)}, u32[]{:S(2)}) copy-start(s32[4,8,1]{1,2,0:T(1,128)} %param.21) | copy-start | bytes 388
  538.3 96.0 %collective-permute-start.7 = (f32[31,64,128]{2,1,0:T(8,128)S(1)}, f32[31,64,128]{2,1,0:T(8,128)}, u32[]{:S(2)}, u32[]{:S(2)}) collective-permute-start(f32[31,64,128]{2,1,0:T(8,128)S(1)} %copy.164), channel_id=1, source_target_pairs={{1,0},{3,2},{5,4},{7,6},{9,8},{11,10},{13,12},{15,14},{17,16},{19,... | collective-permute-start | bytes 3047432 | tf_op jit(solution)/shard_map/ppermute | solution.py:29
  541.2 95.0 %collective-permute-start.6 = (f32[31,64,128]{2,1,0:T(8,128)}, f32[31,64,128]{2,1,0:T(8,128)}, u32[]{:S(2)}, u32[]{:S(2)}) collective-permute-start(f32[31,64,128]{2,1,0:T(8,128)} %copy.163), channel_id=1, source_target_pairs={{0,1},{2,3},{4,5},{6,7},{8,9},{10,11},{12,13},{14,15},{16,17},{18,... | collective-permute-start | bytes 3047432 | tf_op jit(solution)/shard_map/ppermute | solution.py:27
  640.9 187.1 %all-reduce.10.cloned.1.call-start = ((), (), s32[]{:S(2)}) async-start(), calls=%async_computation.9 | async-start | bytes 2097152 | tf_op jit(solution)/shard_map/psum | solution.py:126
  724.7 5.1 collective-permute-start.9
  726.0 5.3 collective-permute-start.8
  729.8 2.1 copy-start.2
  729.8 2.1 copy-start.4
  774.2 5.1 collective-permute-start.11
  776.1 5.3 collective-permute-start.10
  (1 other events, 1.9 us)
Sparse Core Ops, SparseCore 0:
  641.0 43.2 all-reduce.7
  785.0 42.9 all-reduce.9
where the time goes:
time: 848 us; the launch traced here: 838 us
  other arithmetic  275 us (32%)
  local copies, waits for them, and re-layouts  269 us (32%)
  waiting for transfers between devices  110 us (13%)
  blocking collectives  69 us (8%)
  starting transfers between devices  64.8 us (8%)
  matrix products  21.8 us (3%)
  between operations  20.4 us (2%)
    add x378, other arithmetic, add_tap(): return summed + jnp.where(offsets == tap_index, kern[tap_index], 0.0)  261 us
    dynamic_slice x378, local copies, waits for them, and re-layouts, add_tap(): return summed + jnp.where(offsets == tap_index, kern[tap_index], 0.0)  244 us
    psum x2, waiting for transfers between devices, on_device(): total = lax.psum(term, 'view')  86.5 us
    all_to_all x2, blocking collectives, along_rows(): return lax.all_to_all(out, 'xy', split_axis=1, concat_axis=0, tiled=True)  36.9 us
    all_to_all x2, blocking collectives, along_rows(): lax.all_to_all(shortened(vol), 'xy', split_axis=0, concat_axis=1, tiled=T...  32.1 us
    ppermute x6, starting transfers between devices, extended(): lax.ppermute(tail, axis, [(i, (i + 1) % count) for i in range(ends)])  24.3 us
    all_to_all x2, starting transfers between devices, along_rows(): lax.all_to_all(shortened(vol), 'xy', split_axis=0, concat_axis=1, tiled=T...  18.1 us
  transfers between devices with their start and end apart: 18, of which 7 were waited for; matrix products, arithmetic and copies ran while one was open for 63% of the time, Pallas kernels for 0%

commit v1 on v0

--- a/solution.py
+++ b/solution.py
@@ -123,7 +123,7 @@
         back = along_rows(back, mats[1][1], half)
         back = along_planes(back, mats[1][3], half)
         term = mine[None] * back
-        total = lax.psum(term, "view")
+        total = jnp.sum(lax.all_gather(term, "view"), axis=0)
         field = field * total / count[None]
     return field
 

time: 848 us -> 819 us (0.966)
  other arithmetic: 275 us -> 254 us
  local copies, waits for them, and re-layouts: 269 us -> 249 us
    all_gather x0 -> x2, waiting for transfers between devices: none -> 90.3 us  [on_device(): total = jnp.sum(lax.all_gather(term, 'view'), axis=0)]
    psum x2 -> x0, waiting for transfers between devices: 86.5 us -> none  [on_device(): total = lax.psum(term, 'view')]
    add x378, other arithmetic: 261 us -> 236 us  [add_tap(): return summed + jnp.where(offsets == tap_index, kern[tap_index], 0.0)]
    dynamic_slice x378, local copies, waits for them, and re-layouts: 244 us -> 223 us  [add_tap(): return summed + jnp.where(offsets == tap_index, kern[tap_index], 0.0)]
  transfers between devices with their start and end apart: 18 -> 18, of which waited for: 7 -> 7; matrix products, arithmetic and copies ran while one was open for 63% -> 60% of each run, Pallas kernels for 0% -> 0%
where the time goes in v1:
time: 819 us; the launch traced here: 805 us
  other arithmetic  254 us (31%)
  local copies, waits for them, and re-layouts  249 us (30%)
  waiting for transfers between devices  114 us (14%)
  blocking collectives  72.5 us (9%)
  starting transfers between devices  64.7 us (8%)
  matrix products  21.8 us (3%)
  between operations  20.2 us (2%)
  loops' own time  8.38 us (1%)
    add x378, other arithmetic, add_tap(): return summed + jnp.where(offsets == tap_index, kern[tap_index], 0.0)  236 us
    dynamic_slice x378, local copies, waits for them, and re-layouts, add_tap(): return summed + jnp.where(offsets == tap_index, kern[tap_index], 0.0)  223 us
    all_gather x2, waiting for transfers between devices, on_device(): total = jnp.sum(lax.all_gather(term, 'view'), axis=0)  90.3 us
    all_to_all x2, blocking collectives, along_rows(): return lax.all_to_all(out, 'xy', split_axis=1, concat_axis=0, tiled=True)  39 us
    all_to_all x2, blocking collectives, along_rows(): lax.all_to_all(shortened(vol), 'xy', split_axis=0, concat_axis=1, tiled=T...  33.5 us
    ppermute x6, starting transfers between devices, extended(): lax.ppermute(tail, axis, [(i, (i + 1) % count) for i in range(ends)])  23.9 us
    all_to_all x2, starting transfers between devices, along_rows(): lax.all_to_all(shortened(vol), 'xy', split_axis=0, concat_axis=1, tiled=T...  18.1 us
  transfers between devices with their start and end apart: 18, of which 7 were waited for; matrix products, arithmetic and copies ran while one was open for 60% of the time, Pallas kernels for 0%

profile of v1, /device:TPU:0, one launch (start us, length us, event | category | flops | bytes accessed | tf_op | source)
XLA Modules:
  0.0 804.8 jit_solution(8479313486725711573)
XLA Ops:
  9.3 3.9 collective-permute-start
  15.2 74.9 %while.88 = (s32[]{:T(128)}, f32[128,128]{1,0:T(8,128)S(1)}, f32[63]{0:T(128)S(1)}, s32[]{:T(128)}, s32[]{:T(128)}) while((s32[]{:T(128)}, f32[128,128]{1,0:T(8,128)S(1)}, f32[63]{0:T(128)S(1)}, s32[]{:T(128)}, s32[]{:T(128)}) %tuple.181), condition=%wide.region_10.11_spmd.clone, body=%wide.region_9.10_spmd.clone.sunk | while | flops 98307 | bytes 131171 | solution.py:44
  91.9 8.2 %all-to-all-start = ((bf16[32,64,128]{2,1,0:T(8,128)(2,1)}), bf16[32,64,128]{2,1,0:T(8,128)(2,1)S(1)}, u32[]{:S(2)}, u32[]{:S(2)}) async-start(bf16[32,64,128]{2,1,0:T(8,128)(2,1)} %fusion.48), calls=%async_computation | async-start | bytes 1048576 | tf_op jit(solution)/shard_map/all_to_all | solution.py:69
  100.1 80.0 %while.87 = (s32[]{:T(128)}, f32[190,128]{1,0:T(8,128)S(1)}, f32[63]{0:T(128)S(1)}, s32[]{:T(128)}, s32[]{:T(128)}) while((s32[]{:T(128)}, f32[190,128]{1,0:T(8,128)S(1)}, f32[63]{0:T(128)S(1)}, s32[]{:T(128)}, s32[]{:T(128)}) %tuple.184), condition=%wide.region_8.9_spmd.clone, body=%wide.region_7.8_spmd.clone.sunk | while | flops 121603 | bytes 194659 | solution.py:44
  180.2 79.5 %while.89 = (s32[]{:T(128)}, f32[128,128]{1,0:T(8,128)S(1)}, f32[63]{0:T(128)S(1)}, s32[]{:T(128)}, s32[]{:T(128)}) while((s32[]{:T(128)}, f32[128,128]{1,0:T(8,128)S(1)}, f32[63]{0:T(128)S(1)}, s32[]{:T(128)}, s32[]{:T(128)}) %tuple.205), condition=%wide.region_12.13_spmd.clone, body=%wide.region_11.12_spmd.clone.sunk | while | flops 98307 | bytes 131171 | solution.py:44
  263.1 7.3 all-to-all-start.1
  270.4 74.3 %while.86 = (s32[]{:T(128)}, f32[94,32]{1,0:T(8,128)S(1)}, f32[63]{0:T(128)S(1)}, s32[]{:T(128)}, s32[]{:T(128)}) while((s32[]{:T(128)}, f32[94,32]{1,0:T(8,128)S(1)}, f32[63]{0:T(128)S(1)}, s32[]{:T(128)}, s32[]{:T(128)}) %tuple.187), condition=%wide.region_6.7_spmd.clone, body=%wide.region_5.6_spmd.clone.sunk | while | flops 15043 | bytes 24163 | solution.py:44
  354.8 5.5 collective-permute-start.2
  362.0 3.3 collective-permute-start.4
  367.0 5.9 collective-permute-done.3
  374.2 5.6 fusion.68
  386.0 10.0 %all-to-all-start.2 = ((bf16[32,64,128]{2,1,0:T(8,128)(2,1)}), bf16[32,64,128]{2,1,0:T(8,128)(2,1)S(1)}, u32[]{:S(2)}, u32[]{:S(2)}) async-start(bf16[32,64,128]{2,1,0:T(8,128)(2,1)} %convolution_convert_fusion.2), calls=%async_computation.2 | async-start | bytes 1048576 | tf_op jit(solution)/shard_map/all_to_all | solution.py:69
  396.0 80.0 %while.85 = (s32[]{:T(128)}, f32[190,128]{1,0:T(8,128)S(1)}, f32[63]{0:T(128)S(1)}, s32[]{:T(128)}, s32[]{:T(128)}) while((s32[]{:T(128)}, f32[190,128]{1,0:T(8,128)S(1)}, f32[63]{0:T(128)S(1)}, s32[]{:T(128)}, s32[]{:T(128)}) %tuple.203), condition=%wide.region_4.5_spmd.clone, body=%wide.region_3.4_spmd.clone.sunk | while | flops 121603 | bytes 194659 | solution.py:44
  479.3 7.4 all-to-all-start.3
  486.9 13.8 %all-to-all-done.3 = f32[2,1024,128]{2,0,1:T(2,128)S(1)} async-done(((f32[2,1024,128]{2,0,1:T(2,128)}), f32[2,1024,128]{2,0,1:T(2,128)S(1)}, u32[]{:S(2)}, u32[]{:S(2)}) %all-to-all-start.3) | async-done | bytes 1048608 | tf_op jit(solution)/shard_map/all_to_all | solution.py:75
  505.0 4.9 collective-permute-start.6
  509.9 78.9 %while.84 = (s32[]{:T(128)}, f32[94,32]{1,0:T(8,128)S(1)}, f32[63]{0:T(128)S(1)}, s32[]{:T(128)}, s32[]{:T(128)}) while((s32[]{:T(128)}, f32[94,32]{1,0:T(8,128)S(1)}, f32[63]{0:T(128)S(1)}, s32[]{:T(128)}, s32[]{:T(128)}) %tuple.204), condition=%wide.region_2.3_spmd.clone, body=%wide.region_1.2_spmd.clone.sunk | while | flops 15043 | bytes 24163 | solution.py:44
  596.4 45.5 %all-gather.5.cloned.1.call-done = f32[128,64,128]{2,0,1:T(8,128)} async-done(((f32[32,64,128]{2,0,1:T(8,128)}), f32[128,64,128]{2,0,1:T(8,128)}) %all-gather.5.cloned.1.call-update) | async-done | bytes 4194320 | tf_op jit(solution)/shard_map/all_gather | solution.py:126
  647.7 18.6 %all_to_all.108 = bf16[32,64,128]{2,1,0:T(8,128)(2,1)S(1)} all-to-all(bf16[32,64,128]{2,1,0:T(8,128)(2,1)S(1)} %convolution_convert_fusion.1), channel_id=1, replica_groups=mesh['view'=4,'xy'=16,'gz'=2] {'xy'}, dimensions={0} | all-to-all | bytes 1048576 | tf_op jit(solution)/shard_map/all_to_all | solution.py:69
  668.6 19.2 %all_to_all.109 = f32[2,1024,128]{2,0,1:T(2,128)S(1)} all-to-all(f32[2,1024,128]{2,0,1:T(2,128)S(1)} %copy.169), channel_id=1, replica_groups=mesh['view'=4,'xy'=16,'gz'=2] {'xy'}, dimensions={1} | all-to-all | bytes 2097152 | tf_op jit(solution)/shard_map/all_to_all | solution.py:75
  689.4 3.2 collective-permute-start.8
  699.0 15.0 %all_to_all.110 = bf16[32,64,128]{2,1,0:T(8,128)(2,1)S(1)} all-to-all(bf16[32,64,128]{2,1,0:T(8,128)(2,1)S(1)} %convolution_convert_fusion), channel_id=1, replica_groups=mesh['view'=4,'xy'=16,'gz'=2] {'xy'}, dimensions={0} | all-to-all | bytes 1048576 | tf_op jit(solution)/shard_map/all_to_all | solution.py:69
  716.3 19.8 %all_to_all.111 = f32[2,1024,128]{2,0,1:T(2,128)S(1)} all-to-all(f32[2,1024,128]{2,0,1:T(2,128)S(1)} %copy.185), channel_id=1, replica_groups=mesh['view'=4,'xy'=16,'gz'=2] {'xy'}, dimensions={1} | all-to-all | bytes 2097152 | tf_op jit(solution)/shard_map/all_to_all | solution.py:75
  748.2 44.9 %all-gather.7.cloned.1.call-done = f32[128,64,128]{2,0,1:T(8,128)} async-done(((f32[32,64,128]{2,0,1:T(8,128)}), f32[128,64,128]{2,0,1:T(8,128)}) %all-gather.7.cloned.1.call-update) | async-done | bytes 4194320 | tf_op jit(solution)/shard_map/all_gather | solution.py:126
  (908 shorter events, 534.5 us)
Async XLA Ops:
  6.5 83.6 %copy-start = (f32[32,64,128]{2,1,0:T(8,128)S(1)}, f32[32,64,128]{2,1,0:T(8,128)}, u32[]{:S(2)}) copy-start(f32[32,64,128]{2,1,0:T(8,128)} %param.17) | copy-start | bytes 3145732
  8.0 343.1 %collective-permute-start.1 = (bf16[32,64,128]{2,0,1:T(8,128)(2,1)S(1)}, bf16[32,64,128]{2,0,1:T(8,128)(2,1)S(1)}, u32[]{:S(2)}, u32[]{:S(2)}) collective-permute-start(bf16[32,64,128]{2,0,1:T(8,128)(2,1)S(1)} %bitcast.356), channel_id=1, source_target_pairs={{1,0},{3,2},{5,4},{7,6},{9,8},{11,10},{13,12},{15,14},{17,16},{19,... | collective-permute-start | bytes 1572872 | tf_op jit(solution)/shard_map/ppermute | solution.py:29
  9.3 341.8 %collective-permute-start = (bf16[32,64,128]{2,0,1:T(8,128)(2,1)S(1)}, bf16[32,64,128]{2,0,1:T(8,128)(2,1)}, u32[]{:S(2)}, u32[]{:S(2)}) collective-permute-start(bf16[32,64,128]{2,0,1:T(8,128)(2,1)S(1)} %bitcast.357), channel_id=1, source_target_pairs={{0,1},{2,3},{4,5},{6,7},{8,9},{10,11},{12,13},{14,15},{16,17},{18,... | collective-permute-start | bytes 1572872 | tf_op jit(solution)/shard_map/ppermute | solution.py:27
  91.9 167.8 %all-to-all-start = ((bf16[32,64,128]{2,1,0:T(8,128)(2,1)}), bf16[32,64,128]{2,1,0:T(8,128)(2,1)S(1)}, u32[]{:S(2)}, u32[]{:S(2)}) async-start(bf16[32,64,128]{2,1,0:T(8,128)(2,1)} %fusion.48), calls=%async_computation | async-start | bytes 1048576 | tf_op jit(solution)/shard_map/all_to_all | solution.py:69
  263.1 81.7 %copy-start.8 = (s32[1,3]{1,0:T(1,128)S(1)}, s32[1,3]{1,0:T(1,128)}, u32[]{:S(2)}) copy-start(s32[1,3]{1,0:T(1,128)} %param.19) | copy-start | bytes 40
  263.1 97.2 %all-to-all-start.1 = ((f32[2,1024,128]{2,0,1:T(2,128)}), f32[2,1024,128]{2,0,1:T(2,128)S(1)}, u32[]{:S(2)}, u32[]{:S(2)}) async-start(f32[2,1024,128]{2,0,1:T(2,128)} %copy.136), calls=%async_computation.1 | async-start | bytes 2097152 | tf_op jit(solution)/shard_map/all_to_all | solution.py:75
  344.8 36.8 %copy-start.1 = (f32[94,32]{1,0:T(8,128)}, f32[94,32]{1,0:T(8,128)S(1)}, u32[]{:S(2)}) copy-start(f32[94,32]{1,0:T(8,128)S(1)} %get-tuple-element.481) | copy-start | bytes 36100
  353.6 19.4 %collective-permute-start.3 = (bf16[96,32,128]{2,0,1:T(8,128)(2,1)}, bf16[96,32,128]{2,0,1:T(8,128)(2,1)}, u32[]{:S(2)}, u32[]{:S(2)}) collective-permute-start(bf16[96,32,128]{2,0,1:T(8,128)(2,1)} %get-tuple-element.606), channel_id=1, source_target_pairs={{2,0},{4,2},{6,4},{8,6},{10,8},{12,10},{14,12},{16,14},{18,16},{20... | collective-permute-start | bytes 2359304 | tf_op jit(solution)/shard_map/ppermute | solution.py:29
  354.8 19.3 %collective-permute-start.2 = (bf16[96,32,128]{2,0,1:T(8,128)(2,1)}, bf16[96,32,128]{2,0,1:T(8,128)(2,1)}, u32[]{:S(2)}, u32[]{:S(2)}) collective-permute-start(bf16[96,32,128]{2,0,1:T(8,128)(2,1)} %get-tuple-element.605), channel_id=1, source_target_pairs={{0,2},{2,4},{4,6},{6,8},{8,10},{10,12},{12,14},{14,16},{16,18},{18... | collective-permute-start | bytes 2359304 | tf_op jit(solution)/shard_map/ppermute | solution.py:27
  360.7 19.6 %collective-permute-start.5 = (f32[31,64,128]{2,1,0:T(8,128)S(1)}, f32[31,64,128]{2,1,0:T(8,128)S(1)}, u32[]{:S(2)}, u32[]{:S(2)}) collective-permute-start(f32[31,64,128]{2,1,0:T(8,128)S(1)} %get-tuple-element.614), channel_id=1, source_target_pairs={{1,0},{3,2},{5,4},{7,6},{9,8},{11,10},{13,12},{15,14},{17,16},{19,... | collective-permute-start | bytes 3047432 | tf_op jit(solution)/shard_map/ppermute | solution.py:29
  362.0 19.0 %collective-permute-start.4 = (f32[31,64,128]{2,1,0:T(8,128)S(1)}, f32[31,64,128]{2,1,0:T(8,128)S(1)}, u32[]{:S(2)}, u32[]{:S(2)}) collective-permute-start(f32[31,64,128]{2,1,0:T(8,128)S(1)} %get-tuple-element.613), channel_id=1, source_target_pairs={{0,1},{2,3},{4,5},{6,7},{8,9},{10,11},{12,13},{14,15},{16,17},{18,... | collective-permute-start | bytes 3047432 | tf_op jit(solution)/shard_map/ppermute | solution.py:27
  386.0 90.0 %all-to-all-start.2 = ((bf16[32,64,128]{2,1,0:T(8,128)(2,1)}), bf16[32,64,128]{2,1,0:T(8,128)(2,1)S(1)}, u32[]{:S(2)}, u32[]{:S(2)}) async-start(bf16[32,64,128]{2,1,0:T(8,128)(2,1)} %convolution_convert_fusion.2), calls=%async_computation.2 | async-start | bytes 1048576 | tf_op jit(solution)/shard_map/all_to_all | solution.py:69
  479.3 7.5 copy-start.7
  479.3 21.4 %all-to-all-start.3 = ((f32[2,1024,128]{2,0,1:T(2,128)}), f32[2,1024,128]{2,0,1:T(2,128)S(1)}, u32[]{:S(2)}, u32[]{:S(2)}) async-start(f32[2,1024,128]{2,0,1:T(2,128)} %copy.152), calls=%async_computation.3 | async-start | bytes 2097152 | tf_op jit(solution)/shard_map/all_to_all | solution.py:75
  486.8 155.1 %all-gather.5.cloned.1.call-start = ((), (), s32[]{:S(2)}) async-start(), calls=%async_computation.8 | async-start | bytes 5242880 | tf_op jit(solution)/shard_map/all_gather | solution.py:126
  502.1 86.7 %copy-start.6 = (s32[4,8,1]{1,2,0:T(1,128)S(1)}, s32[4,8,1]{1,2,0:T(1,128)}, u32[]{:S(2)}) copy-start(s32[4,8,1]{1,2,0:T(1,128)} %param.21) | copy-start | bytes 388
  502.1 87.6 %collective-permute-start.7 = (f32[31,64,128]{2,1,0:T(8,128)S(1)}, f32[31,64,128]{2,1,0:T(8,128)}, u32[]{:S(2)}, u32[]{:S(2)}) collective-permute-start(f32[31,64,128]{2,1,0:T(8,128)S(1)} %copy.155), channel_id=1, source_target_pairs={{1,0},{3,2},{5,4},{7,6},{9,8},{11,10},{13,12},{15,14},{17,16},{19,... | collective-permute-start | bytes 3047432 | tf_op jit(solution)/shard_map/ppermute | solution.py:29
  505.0 86.6 %collective-permute-start.6 = (f32[31,64,128]{2,1,0:T(8,128)}, f32[31,64,128]{2,1,0:T(8,128)}, u32[]{:S(2)}, u32[]{:S(2)}) collective-permute-start(f32[31,64,128]{2,1,0:T(8,128)} %copy.154), channel_id=1, source_target_pairs={{0,1},{2,3},{4,5},{6,7},{8,9},{10,11},{12,13},{14,15},{16,17},{18,... | collective-permute-start | bytes 3047432 | tf_op jit(solution)/shard_map/ppermute | solution.py:27
  596.3 196.8 %all-gather.7.cloned.1.call-start = ((), (), s32[]{:S(2)}) async-start(), calls=%async_computation.9 | async-start | bytes 5242880 | tf_op jit(solution)/shard_map/all_gather | solution.py:126
  688.1 5.1 collective-permute-start.9
  689.4 5.3 collective-permute-start.8
  737.5 5.1 collective-permute-start.11
  739.4 5.3 collective-permute-start.10
  793.1 2.8 copy-start.5
  (3 other events, 6.1 us)
Sparse Core Ops, SparseCore 0:
  596.4 45.3 all-gather.4
  748.4 44.6 all-gather.6
